TPU v7x, 1024 devices: a whole 8x8x8 slice. The times are simulated.
1024 devices in a mesh: hi: 64 (over z_lo, y, core), lo: 16 (over x, z_hi).
Axes of the slice: x: 8, y: 8, z: 8 (z_hi: 2, z_lo: 4; z = z_hi * 4 + z_lo), core: 2. Of those that a mesh axis runs over, the one named last changes fastest.
Arguments:
- state: float32 [2, 33554432], P(None, ('hi', 'lo')), may hold values from -15 to 15
- gates: float32 [16, 2, 128, 128], replicated, may hold values from -1 to 1, as said below
- remap_perm: int32 [16], replicated, may hold values from 0 to 15, each once
Outputs:
- final_state: float32 [2, 33554432], P(None, ('hi', 'lo'))
Inputs may be any that keep to these rules, and one draw needn't show every extreme that they name: Each gates[g] is a unitary matrix (real part gates[g][0], imaginary part gates[g][1]) up to float32 rounding.
All inputs are finite; a program needn't handle non-finite values.
Results may differ from a plain program's by a relative error of at most 0.00016.
Values sent between devices are 32-bit elements; how exact they have to be, the bound alone decides.
A program may use at most 32 MiB of HBM per device.

v0:
```python
import jax
import jax.numpy as jnp
from jax import lax
from jax.sharding import PartitionSpec as P


def swapped(value, axis, distance):
    mask = 2**distance
    pairs = [(source, source ^ mask) for source in range(lax.axis_size(axis))]
    return lax.ppermute(value, axis, pairs)


def apply_last(blocks, gate):

    def contract(data, matrix):
        return jnp.einsum("...j,ij->...i", data, matrix, precision=lax.Precision.HIGHEST)

    real_out = contract(blocks[0], gate[0]) - contract(blocks[1], gate[1])
    imag_out = contract(blocks[0], gate[1]) + contract(blocks[1], gate[0])
    return jnp.stack([real_out, imag_out])


def apply_mid(blocks, gate):

    def contract(data, matrix):
        return jnp.einsum("ij,ajb->aib", matrix, data, precision=lax.Precision.HIGHEST)

    real_out = contract(blocks[0], gate[0]) - contract(blocks[1], gate[1])
    imag_out = contract(blocks[0], gate[1]) + contract(blocks[1], gate[0])
    return jnp.stack([real_out, imag_out])


def apply_gate(vector, gate, low):
    count = vector.shape[1]
    order = gate.shape[-1]
    if low == 0:
        return apply_last(vector.reshape(2, count // order, order), gate).reshape(2, count)
    width = 1 << low
    shaped = vector.reshape(2, count // (order * width), order, width)
    return apply_mid(shaped, gate).reshape(2, count)


def run_group(vector, gates, group, first):
    qubits = vector.shape[1].bit_length() - 1
    gate_bits = gates.shape[-1].bit_length() - 1
    starts = [0, qubits - gate_bits, qubits - gate_bits - 1, 0]
    for layer in range(first, 4):
        vector = apply_gate(vector, gates[4 * group + layer], starts[layer])
    return vector


def partner(vector, bit):
    halves = vector.reshape(2, 2, vector.shape[1] // 2)
    low_side = lax.axis_index("hi") >> bit & 1 == 0
    outgoing = jnp.where(low_side, halves[:, 1], halves[:, 0])
    kept = jnp.where(low_side, halves[:, 0], halves[:, 1])
    arrived = swapped(outgoing, "hi", bit)
    return (kept, arrived, low_side)


def assemble(kept, arrived, low_side):
    first_half = jnp.where(low_side, kept, arrived)
    second_half = jnp.where(low_side, arrived, kept)
    return jnp.concatenate([first_half, second_half], axis=1)


def per_device(state, gates, remap_perm):
    top_bit = lax.axis_size("hi").bit_length() - 1
    vector = run_group(state, gates, 0, 0)
    for group, bit in ((1, top_bit - 2), (2, 0)):
        kept, arrived, low_side = partner(vector, bit)
        vector = run_group(assemble(kept, arrived, low_side), gates, group, 0)
    block_count = lax.axis_size("lo")
    order = gates.shape[-1]
    shaped = vector.reshape(2, block_count, -1)
    one_hot = (remap_perm[None, :] == jnp.arange(block_count, dtype=jnp.int32)[:, None]).astype(
        jnp.float32
    )
    shaped = jnp.einsum("jb,xbr->xjr", one_hot, shaped, precision=lax.Precision.HIGHEST)
    shaped = shaped.reshape(2, block_count, -1, order)
    vector = apply_last(
        lax.all_to_all(shaped, "lo", split_axis=1, concat_axis=1, tiled=True), gates[12]
    ).reshape(2, -1)
    vector = run_group(vector, gates, 3, 1)
    kept, arrived, low_side = partner(vector, top_bit // 2)
    vector = assemble(kept, arrived, low_side)
    total = lax.psum(jnp.sum(vector * vector), ("hi", "lo"))
    mean_sq = total / (2 * vector.shape[1] * lax.axis_size("hi") * lax.axis_size("lo"))
    return vector / jnp.sqrt(mean_sq + 1e-06)


def solution(mesh):
    in_specs = (P(None, ("hi", "lo")), P(), P())
    out_specs = P(None, ("hi", "lo"))
    return jax.shard_map(
        per_device, mesh=mesh, in_specs=in_specs, out_specs=out_specs, check_vma=False
    )
```

profile of v0, /device:TPU:1, one launch (start us, length us, event | category | flops | bytes accessed | tf_op | source)
XLA Modules:
  0.0 205.4 jit_solution(6214632842927772449)
XLA Ops:
  0.0 1.4 fusion.183
  1.4 1.1 fusion.107
  2.5 1.1 fusion.111
  3.7 1.1 convolution_subtract_fusion.15
  4.8 1.2 fusion.101
  6.1 0.4 fusion.105
  6.5 0.3 convolution_add_fusion.15
  6.8 0.4 fusion.7
  7.9 0.4 fusion.6
  8.4 0.3 convolution_subtract_fusion.13
  8.7 0.3 fusion.89
  8.9 0.3 fusion.99
  9.5 0.3 convolution_add_fusion.12
  9.9 0.3 convolution_subtract_fusion.12
  10.7 5.7 %collective-permute-start = (f32[2,16384]{1,0:T(2,128)S(1)}, f32[2,16384]{1,0:T(2,128)S(1)}, u32[]{:S(2)}, u32[]{:S(2)}) collective-permute-start(f32[2,16384]{1,0:T(2,128)S(1)} %bitcast.381), channel_id=1, source_target_pairs={{0,256},{16,272},{32,288},{48,304},{64,320},{80,336},{96,352},{112... | collective-permute-start | bytes 393224 | tf_op jit(solution)/shard_map/ppermute | solution.py:10
  16.4 2.3 %collective-permute-done = f32[2,16384]{1,0:T(2,128)S(1)} collective-permute-done((f32[2,16384]{1,0:T(2,128)S(1)}, f32[2,16384]{1,0:T(2,128)S(1)}, u32[]{:S(2)}, u32[]{:S(2)}) %collective-permute-start) | collective-permute-done | bytes 131104 | tf_op jit(solution)/shard_map/ppermute | solution.py:10
  19.2 0.3 fusion.83
  19.5 0.3 fusion.87
  19.7 0.3 convolution_subtract_fusion.11
  20.1 0.4 fusion.77
  20.5 0.4 fusion.81
  20.9 0.3 convolution_add_fusion.11
  21.2 0.4 fusion.5
  22.3 0.4 fusion.4
  23.1 0.3 fusion.65
  23.3 0.3 fusion.75
  23.9 0.3 convolution_add_fusion.8
  24.3 0.3 convolution_subtract_fusion.8
  25.0 15.0 %collective-permute-start.1 = (f32[2,16384]{1,0:T(2,128)S(1)}, f32[2,16384]{1,0:T(2,128)S(1)}, u32[]{:S(2)}, u32[]{:S(2)}) collective-permute-start(f32[2,16384]{1,0:T(2,128)S(1)} %bitcast.382), channel_id=1, source_target_pairs={{0,16},{16,0},{32,48},{48,32},{64,80},{80,64},{96,112},{112,96},{1... | collective-permute-start | bytes 393224 | tf_op jit(solution)/shard_map/ppermute | solution.py:10
  40.0 0.8 collective-permute-done.1
  41.2 0.3 fusion.59
  41.5 0.3 fusion.63
  41.8 0.3 convolution_subtract_fusion.7
  42.1 0.4 fusion.53
  42.5 0.4 fusion.57
  42.9 0.3 convolution_add_fusion.7
  43.3 0.4 fusion.3
  44.3 0.4 fusion.2
  44.8 0.3 convolution_subtract_fusion.5
  45.1 0.3 fusion.51
  45.4 0.3 fusion.41
  46.0 0.3 convolution_subtract_fusion.4
  46.3 0.3 convolution_add_fusion.4
  46.9 0.7 copy.46
  47.7 7.0 %all-to-all-start = ((f32[2,16,16,128]{3,2,0,1:T(8,128)}), f32[2,16,16,128]{3,2,0,1:T(8,128)S(1)}, u32[]{:S(2)}, u32[]{:S(2)}) async-start(f32[2,16,16,128]{3,2,0,1:T(8,128)} %copy.46), calls=%async_computation | async-start | bytes 524288 | tf_op jit(solution)/shard_map/all_to_all | solution.py:82
  54.7 14.9 %all-to-all-done = f32[2,16,16,128]{3,2,0,1:T(8,128)S(1)} async-done(((f32[2,16,16,128]{3,2,0,1:T(8,128)}), f32[2,16,16,128]{3,2,0,1:T(8,128)S(1)}, u32[]{:S(2)}, u32[]{:S(2)}) %all-to-all-start) | async-done | bytes 262176 | tf_op jit(solution)/shard_map/all_to_all | solution.py:82
  69.6 0.3 fusion.18
  69.9 0.3 convolution_subtract_fusion.3
  70.2 0.4 fusion.31
  70.6 0.4 fusion.39
  71.0 0.3 fusion.17
  71.3 0.3 convolution_add_fusion.3
  71.6 0.4 fusion.1
  72.7 0.4 fusion
  73.2 0.3 convolution_subtract_fusion.1
  73.5 0.3 fusion.29
  73.8 0.3 fusion.19
  74.3 0.3 convolution_subtract_fusion
  74.6 0.3 convolution_add_fusion
  75.1 7.9 %collective-permute-start.2 = (f32[2,16384]{1,0:T(2,128)S(1)}, f32[2,16384]{1,0:T(2,128)S(1)}, u32[]{:S(2)}, u32[]{:S(2)}) collective-permute-start(f32[2,16384]{1,0:T(2,128)S(1)} %select_bitcast_fusion), channel_id=1, source_target_pairs={{0,128},{16,144},{32,160},{48,176},{64,192},{80,208},{96,224},{112... | collective-permute-start | bytes 393224 | tf_op jit(solution)/shard_map/ppermute | solution.py:10
  83.0 2.4 %collective-permute-done.2 = f32[2,16384]{1,0:T(2,128)S(1)} collective-permute-done((f32[2,16384]{1,0:T(2,128)S(1)}, f32[2,16384]{1,0:T(2,128)S(1)}, u32[]{:S(2)}, u32[]{:S(2)}) %collective-permute-start.2) | collective-permute-done | bytes 131104 | tf_op jit(solution)/shard_map/ppermute | solution.py:10
  85.7 0.9 multiply_reduce_fusion
  86.6 117.3 %psum.7 = f32[]{:T(128)} all-reduce(f32[]{:T(128)} %multiply_reduce_fusion), channel_id=1, replica_groups=mesh['hi'=64,'lo'=16] {'hi','lo'}, use_global_device_ids=true, to_apply=%region_1.2 | all-reduce | flops 1 | bytes 8 | tf_op jit(solution)/shard_map/psum | solution.py:87
  204.6 0.8 broadcast_divide_fusion
  (63 shorter events, 7.4 us)
Async XLA Ops:
  0.0 6.1 %copy-start = (f32[16,2,128,128]{3,2,1,0:T(8,128)S(1)}, f32[16,2,128,128]{3,2,1,0:T(8,128)}, u32[]{:S(2)}) copy-start(f32[16,2,128,128]{3,2,1,0:T(8,128)} %param.4) | copy-start | bytes 6291460
  10.7 8.1 %collective-permute-start = (f32[2,16384]{1,0:T(2,128)S(1)}, f32[2,16384]{1,0:T(2,128)S(1)}, u32[]{:S(2)}, u32[]{:S(2)}) collective-permute-start(f32[2,16384]{1,0:T(2,128)S(1)} %bitcast.381), channel_id=1, source_target_pairs={{0,256},{16,272},{32,288},{48,304},{64,320},{80,336},{96,352},{112... | collective-permute-start | bytes 393224 | tf_op jit(solution)/shard_map/ppermute | solution.py:10
  25.0 15.8 %collective-permute-start.1 = (f32[2,16384]{1,0:T(2,128)S(1)}, f32[2,16384]{1,0:T(2,128)S(1)}, u32[]{:S(2)}, u32[]{:S(2)}) collective-permute-start(f32[2,16384]{1,0:T(2,128)S(1)} %bitcast.382), channel_id=1, source_target_pairs={{0,16},{16,0},{32,48},{48,32},{64,80},{80,64},{96,112},{112,96},{1... | collective-permute-start | bytes 393224 | tf_op jit(solution)/shard_map/ppermute | solution.py:10
  44.0 2.6 %copy-start.1 = (s32[16]{0:T(128)S(1)}, s32[16]{0:T(128)}, u32[]{:S(2)}) copy-start(s32[16]{0:T(128)} %param.5) | copy-start | bytes 196
  47.7 21.9 %all-to-all-start = ((f32[2,16,16,128]{3,2,0,1:T(8,128)}), f32[2,16,16,128]{3,2,0,1:T(8,128)S(1)}, u32[]{:S(2)}, u32[]{:S(2)}) async-start(f32[2,16,16,128]{3,2,0,1:T(8,128)} %copy.46), calls=%async_computation | async-start | bytes 524288 | tf_op jit(solution)/shard_map/all_to_all | solution.py:82
  75.1 10.3 %collective-permute-start.2 = (f32[2,16384]{1,0:T(2,128)S(1)}, f32[2,16384]{1,0:T(2,128)S(1)}, u32[]{:S(2)}, u32[]{:S(2)}) collective-permute-start(f32[2,16384]{1,0:T(2,128)S(1)} %select_bitcast_fusion), channel_id=1, source_target_pairs={{0,128},{16,144},{32,160},{48,176},{64,192},{80,208},{96,224},{112... | collective-permute-start | bytes 393224 | tf_op jit(solution)/shard_map/ppermute | solution.py:10
where the time goes:
time: 206 us; the launch traced here: 205 us
  blocking collectives  117 us (57%)
  starting transfers between devices  35.6 us (17%)
  matrix products  23 us (11%)
  waiting for transfers between devices  20.5 us (10%)
  local copies, waits for them, and re-layouts  3.97 us (2%)
  other arithmetic  3.47 us (2%)
    psum x1, blocking collectives, per_device(): total = lax.psum(jnp.sum(vector * vector), ('hi', 'lo'))  117 us
    ppermute x3, starting transfers between devices, swapped(): return lax.ppermute(value, axis, pairs)  28.6 us
    all_to_all x1, waiting for transfers between devices, per_device(): lax.all_to_all(shaped, 'lo', split_axis=1, concat_axis=1, tiled=True)  14.9 us
    dot_general x32, matrix products, contract(): jnp.einsum('...j,ij->...i', data, matrix, precision=lax.Precision.HIGHEST)  11.4 us
    dot_general x32, matrix products, contract(): jnp.einsum('ij,ajb->aib', matrix, data, precision=lax.Precision.HIGHEST)  11.3 us
    all_to_all x1, starting transfers between devices, per_device(): lax.all_to_all(shaped, 'lo', split_axis=1, concat_axis=1, tiled=True)  6.98 us
    ppermute x3, waiting for transfers between devices, swapped(): return lax.ppermute(value, axis, pairs)  5.56 us
  transfers between devices with their start and end apart: 4, of which 4 were waited for; matrix products, arithmetic and copies ran while one was open for 0% of the time, Pallas kernels for 0%

commit v1 on v0

v1 whole, which is shorter than its diff:
```python
import functools

import jax
import jax.numpy as jnp
from jax import lax
from jax.experimental import pallas as pl
from jax.experimental.pallas import tpu as pltpu
from jax.sharding import PartitionSpec as P

F32 = jnp.float32
BF16 = jnp.bfloat16
MESH = pl.DeviceIdType.MESH

SWAP_BITS = (4, 0, 3)
NORM_MASKS = [
    (b1 << 1) | (b2 << 2) | (b4 << 4) | (b5 << 5)
    for b5 in (1, 0)
    for b4 in (1, 0)
    for b2 in (1, 0)
    for b1 in (1, 0)
    if b1 or b2 or b4 or b5
]
LO_STEPS = sorted(
    [(dx, dz) for dx in range(8) for dz in range(2) if dx or dz],
    key=lambda s: -(min(s[0], 8 - s[0]) + 4 * s[1]),
)


def bit_of(value, bit):
    return lax.rem(lax.div(value, 1 << bit), 2)


def flipped(value, mask):
    result = value
    for bit in range(6):
        if mask >> bit & 1:
            result = result + (1 - 2 * bit_of(value, bit)) * (1 << bit)
    return result


def split(value):
    high = value.astype(BF16)
    low = (value - high.astype(F32)).astype(BF16)
    return high, low


def gate_matrix(real, imag):
    rh, rl = split(real)
    ih, il = split(imag)
    top = jnp.concatenate([rh, -ih, rl, -il, rh, -ih], axis=1)
    bottom = jnp.concatenate([ih, rh, il, rl, ih, rh], axis=1)
    return top, bottom


def left(matrix, data):
    high, low = split(data)
    stacked = jnp.concatenate([high, high, low], axis=0)
    return jnp.dot(matrix, stacked, preferred_element_type=F32)


def right(data, matrix):
    high, low = split(data)
    stacked = jnp.concatenate([high, high, low], axis=1)
    return lax.dot_general(
        stacked, matrix, (((1,), (1,)), ((), ())), preferred_element_type=F32
    )


def kernel(
    perm_ref, x_hbm, g_hbm, out_ref, norm_ref,
    x, g, mats, work, rmat, prod,
    s1, a1, t1, s2, a2, t2, u2, stage, recv, f3, g3, k3,
    nsrc, nrecv, qsrc, qrecv,
    load_sem, ssem, rsem, nssem, nrsem, assem, arsem, qssem, qrsem,
):
    hi = lax.axis_index("hi")
    lo = lax.axis_index("lo")
    x_at = lax.div(lo, 2)
    z_at = lax.rem(lo, 2)

    def lo_peer(dx, dz):
        zz = z_at + dz * (1 - 2 * z_at)
        return lax.rem(x_at + dx, 8) * 2 + zz

    def hi_id(mask):
        return (flipped(hi, mask), lo)

    load_x = pltpu.make_async_copy(x_hbm, x, load_sem.at[0])
    load_g0 = pltpu.make_async_copy(g_hbm.at[1], g.at[1], load_sem.at[1])
    load_ga = pltpu.make_async_copy(g_hbm.at[0], g.at[0], load_sem.at[2])
    load_gb = pltpu.make_async_copy(g_hbm.at[pl.ds(2, 14)], g.at[pl.ds(2, 14)], load_sem.at[3])
    load_g0.start()
    load_x.start()
    load_gb.start()
    load_ga.start()

    barrier = pltpu.get_barrier_semaphore()
    hi_masks = NORM_MASKS + [1 << SWAP_BITS[1], 1 << SWAP_BITS[2]]
    for dx, dz in LO_STEPS:
        pl.semaphore_signal(
            barrier, inc=1, device_id=(hi, lo_peer(dx, dz)), device_id_type=MESH
        )
    for mask in hi_masks:
        pl.semaphore_signal(barrier, inc=1, device_id=hi_id(mask), device_id_type=MESH)

    def prepare(slot, gate):
        top, bottom = gate_matrix(g[gate, 0], g[gate, 1])
        mats[slot, 0:128, :] = top
        mats[slot, 128:256, :] = bottom

    def exchange(src, dst, index, mask):
        return pltpu.make_async_remote_copy(
            src_ref=src,
            dst_ref=dst,
            send_sem=ssem.at[index],
            recv_sem=rsem.at[index],
            device_id=hi_id(mask),
            device_id_type=MESH,
        )

    load_g0.wait()
    prepare(0, 1)
    load_x.wait()

    values = x[...].reshape(64, 8, 128)
    nsrc[0] = jnp.sum(jnp.sum(values * values, axis=0), axis=0, keepdims=True)

    data = jnp.concatenate(
        [
            jnp.concatenate([x[pl.ds(c, 128, stride=4), :], x[pl.ds(2 + c, 128, stride=4), :]], axis=1)
            for c in range(2)
        ],
        axis=0,
    )
    y = left(mats[0], data)

    def put_rows(ref, result):
        for c in range(2):
            for b in range(2):
                ref[c, pl.ds(b, 128, stride=2), :] = result[
                    c * 128 : (c + 1) * 128, b * 128 : (b + 1) * 128
                ]

    def get_rows(ref):
        return jnp.concatenate(
            [
                jnp.concatenate(
                    [ref[c, pl.ds(0, 128, stride=2), :], ref[c, pl.ds(1, 128, stride=2), :]], axis=1
                )
                for c in range(2)
            ],
            axis=0,
        )

    put_rows(s1, y)
    pl.semaphore_wait(barrier, len(LO_STEPS) + len(hi_masks))

    def half(side):
        return pl.ds(pl.multiple_of(side * 128, 128), 128)

    side = bit_of(hi, SWAP_BITS[0])
    send1 = exchange(s1.at[:, half(1 - side), :], a1, 0, 1 << SWAP_BITS[0])
    send1.start()
    norm_sends = []
    for i, mask in enumerate(NORM_MASKS):
        copy = pltpu.make_async_remote_copy(
            src_ref=nsrc.at[0],
            dst_ref=nrecv.at[i],
            send_sem=nssem.at[i],
            recv_sem=nrsem.at[i],
            device_id=hi_id(mask),
            device_id_type=MESH,
        )
        copy.start()
        norm_sends.append(copy)

    def gate_mid(slot, read, ref, where):
        result = left(mats[slot], jnp.concatenate([read(0), read(1)], axis=0))
        for c in range(2):
            ref[c, where, :] = result[c * 128 : (c + 1) * 128, :]

    load_gb.wait()
    load_ga.wait()
    prepare(1, 2)
    gate_mid(1, lambda c: s1[c, half(side), :], t1, half(side))
    prepare(2, 5)
    prepare(3, 6)
    prepare(4, 9)
    for b in range(2):
        rows = pl.ds(b, 64, stride=2)
        top, bottom = gate_matrix(g.at[10, 0][rows, :], g.at[10, 1][rows, :])
        mats[5, b * 64 : (b + 1) * 64, :] = top
        mats[5, 128 + b * 64 : 128 + (b + 1) * 64, :] = bottom
    prepare(6, 13)
    prepare(7, 14)

    prod[0:128, :] = g[0, 0]
    prod[128:256, :] = g[0, 1]
    for gate in (3, 4, 7, 8, 11, 12, 15):
        top, bottom = gate_matrix(g[gate, 0], g[gate, 1])
        work[0:128, :] = top
        work[128:256, :] = bottom
        prod[...] = left(work[...], prod[...])
    top, bottom = gate_matrix(prod[0:128, :], prod[128:256, :])
    rmat[0:128, :] = top
    rmat[128:256, :] = bottom

    send1.wait()
    gate_mid(1, lambda c: a1[c], t1, half(1 - side))

    put_rows(s2, left(mats[2], get_rows(t1)))
    side = bit_of(hi, SWAP_BITS[1])
    send2 = exchange(s2.at[:, half(1 - side), :], a2, 1, 1 << SWAP_BITS[1])
    send2.start()
    for copy in norm_sends:
        copy.wait()
    total = nsrc[0]
    for i in range(len(NORM_MASKS)):
        total = total + nrecv[i]
    nsrc[1] = total
    nsend2 = exchange(nsrc.at[1], nrecv.at[15], 4, 1 << SWAP_BITS[1])
    nsend2.start()
    gate_mid(3, lambda c: s2[c, half(side), :], t2, half(side))
    send2.wait()
    gate_mid(3, lambda c: a2[c], t2, half(1 - side))
    nsend2.wait()
    qsrc[0] = nsrc[1] + nrecv[15]

    put_rows(t1, left(mats[4], get_rows(t2)))
    data = jnp.concatenate(
        [jnp.concatenate([t1[c, 0:128, :], t1[c, 128:256, :]], axis=1) for c in range(2)], axis=0
    )
    y = left(mats[5], data)
    for c in range(2):
        for b in range(2):
            for t in range(2):
                base = c * 128 + b * 64
                u2[c, b, t * 8 : (t + 1) * 8] = y[
                    base : base + 64, t * 128 : (t + 1) * 128
                ].reshape(8, 8, 128)

    for j in range(16):
        block = jnp.int32(0)
        for v in range(1, 16):
            block = jnp.where(perm_ref[v] == j, v, block)
        for b in range(2):
            for c in range(2):
                stage[b, j, c] = u2[c, b, block]
    sends = [[], []]
    for b in range(2):
        for dx, dz in LO_STEPS:
            peer = lo_peer(dx, dz)
            copy = pltpu.make_async_remote_copy(
                src_ref=stage.at[b, peer],
                dst_ref=recv.at[b, lo],
                send_sem=assem.at[b, dx * 2 + dz],
                recv_sem=arsem.at[b, dx * 2 + dz],
                device_id=(hi, peer),
                device_id_type=MESH,
            )
            copy.start()
            sends[b].append(copy)
    qsends = []
    for dx, dz in LO_STEPS:
        copy = pltpu.make_async_remote_copy(
            src_ref=qsrc.at[0],
            dst_ref=qrecv.at[dx * 2 + dz],
            send_sem=qssem.at[dx * 2 + dz],
            recv_sem=qrsem.at[dx * 2 + dz],
            device_id=(hi, lo_peer(dx, dz)),
            device_id_type=MESH,
        )
        copy.start()
        qsends.append(copy)
    for b in range(2):
        recv[b, lo] = stage[b, lo]

    side = bit_of(hi, SWAP_BITS[2])

    def quarter(which):
        return pl.ds(pl.multiple_of(which * 64, 64), 64)

    sends3 = []
    for b in range(2):
        for copy in sends[b]:
            copy.wait()
        data = jnp.concatenate(
            [recv[b, :, 0].reshape(128, 128), recv[b, :, 1].reshape(128, 128)], axis=0
        )
        y = left(mats[6], data)
        for c in range(2):
            f3[b, c] = y[c * 128 : (c + 1) * 128, :]
        copy = exchange(f3.at[b, :, quarter(1 - side), :], g3.at[b], 2 + b, 1 << SWAP_BITS[2])
        copy.start()
        sends3.append(copy)
    total = qsrc[0]
    for copy in qsends:
        copy.wait()
    for dx, dz in LO_STEPS:
        total = total + qrecv[dx * 2 + dz]
    qsrc[1] = total
    nsend3 = exchange(qsrc.at[1], qrecv.at[0], 5, 1 << SWAP_BITS[2])
    nsend3.start()

    def finish(where):
        y = left(mats[7], jnp.concatenate([k3[0], k3[1]], axis=0))
        y = right(jnp.concatenate([y[0:128, :], y[128:256, :]], axis=1), rmat[...])
        for c in range(2):
            out_ref[pl.ds(where * 256 + c, 128, stride=2), :] = y[:, c * 128 : (c + 1) * 128]

    for b in range(2):
        for c in range(2):
            k3[c, pl.ds(b, 64, stride=2), :] = f3[b, c, quarter(side), :]
    finish(side)
    for b in range(2):
        sends3[b].wait()
        for c in range(2):
            k3[c, pl.ds(b, 64, stride=2), :] = g3[b, c]
    finish(1 - side)
    nsend3.wait()
    norm_ref[...] = qsrc[1] + qrecv[0]


def per_device(count, state, gates, remap_perm):
    rows = state.reshape(2, 256, 128).transpose(1, 0, 2).reshape(512, 128)
    vm = pltpu.VMEM
    dma = pltpu.SemaphoreType.DMA
    out, norm = pl.pallas_call(
        kernel,
        out_shape=(
            jax.ShapeDtypeStruct((512, 128), F32),
            jax.ShapeDtypeStruct((1, 128), F32),
        ),
        in_specs=[
            pl.BlockSpec(memory_space=pltpu.SMEM),
            pl.BlockSpec(memory_space=pl.ANY),
            pl.BlockSpec(memory_space=pl.ANY),
        ],
        out_specs=(
            pl.BlockSpec(memory_space=pltpu.VMEM),
            pl.BlockSpec(memory_space=pltpu.VMEM),
        ),
        scratch_shapes=[
            vm((512, 128), F32),
            vm((16, 2, 128, 128), F32),
            vm((8, 256, 768), BF16),
            vm((256, 768), BF16),
            vm((256, 768), BF16),
            vm((256, 128), F32),
            vm((2, 256, 128), F32),
            vm((2, 128, 128), F32),
            vm((2, 256, 128), F32),
            vm((2, 256, 128), F32),
            vm((2, 128, 128), F32),
            vm((2, 256, 128), F32),
            vm((2, 2, 16, 8, 128), F32),
            vm((2, 16, 2, 8, 128), F32),
            vm((2, 16, 2, 8, 128), F32),
            vm((2, 2, 128, 128), F32),
            vm((2, 2, 64, 128), F32),
            vm((2, 128, 128), F32),
            vm((2, 1, 128), F32),
            vm((16, 1, 128), F32),
            vm((2, 1, 128), F32),
            vm((16, 1, 128), F32),
            dma((4,)),
            dma((6,)),
            dma((6,)),
            dma((15,)),
            dma((15,)),
            dma((2, 16)),
            dma((2, 16)),
            dma((16,)),
            dma((16,)),
        ],
        compiler_params=pltpu.CompilerParams(collective_id=0, has_side_effects=True),
    )(remap_perm, rows, gates)
    mean_sq = jnp.sum(norm) / count
    scaled = out * (1.0 / jnp.sqrt(mean_sq + 1e-06))
    return scaled.reshape(256, 2, 128).transpose(1, 0, 2).reshape(2, 32768)


def solution(mesh):
    devices = mesh.shape["hi"] * mesh.shape["lo"]
    in_specs = (P(None, ("hi", "lo")), P(), P())
    out_specs = P(None, ("hi", "lo"))
    return jax.shard_map(
        functools.partial(per_device, 2.0 * 32768 * devices),
        mesh=mesh,
        in_specs=in_specs,
        out_specs=out_specs,
        check_vma=False,
    )
```

time: 206 us -> 54.1 us (0.26)
  the two profiles are of different devices: /device:TPU:1 before, /device:TPU:2 now
where the time goes in v1:
time: 54.1 us; the launch traced here: 53.9 us
  Pallas kernels  50.2 us (93%)
  other arithmetic  2.94 us (5%)
  between operations  0.7 us (1%)
    pallas_call x1, Pallas kernels, per_device(): pl.pallas_call(kernel, out_shape=(jax.ShapeDtypeStruct((512, 128), F32),...  50.2 us
    mul x1, other arithmetic, per_device(): scaled = out * (1.0 / jnp.sqrt(mean_sq + 1e-06))  1.67 us
    reduce_sum x1, other arithmetic, per_device(): mean_sq = jnp.sum(norm) / count  1.27 us

profile of v1, /device:TPU:2, one launch (start us, length us, event | category | flops | bytes accessed | tf_op | source)
XLA Modules:
  0.0 53.9 jit_solution(2560365974171786749)
XLA Ops:
  0.0 50.2 %shard_map.37 = (f32[512,128]{1,0:T(8,128)}, f32[1,128]{1,0:T(1,128)}) custom-call(s32[16]{0:T(128)} %perm_ref.1, f32[512,128]{1,0:T(8,128)} %bitcast.10, f32[16,2,128,128]{3,2,1,0:T(8,128)} %g_hbm.1), custom_call_target="tpu_custom_call" | custom-call | tf_op jit(solution)/shard_map/pallas_call | solution.py:328
  50.2 1.3 %reduce_sum.9 = f32[]{:T(128)} reduce(f32[1,128]{1,0:T(1,128)} %get-tuple-element.8, f32[]{:T(128)} %constant.3.clone.1), dimensions={0,1}, to_apply=%region_0.0 | reduce | flops 127 | bytes 520 | tf_op jit(solution)/shard_map/reduce_sum | solution.py:378
  52.2 1.7 %broadcast_multiply_fusion = f32[512,128]{1,0:T(8,128)} fusion(f32[512,128]{1,0:T(8,128)} %get-tuple-element.7, f32[]{:T(128)S(6)} %sqrt.3), kind=kLoop, calls=%fused_computation | loop fusion | flops 65536 | bytes 524292 | tf_op jit(solution)/shard_map/mul | solution.py:379

commit v2 on v1

--- a/solution.py
+++ b/solution.py
@@ -12,14 +12,8 @@
 MESH = pl.DeviceIdType.MESH
 
 SWAP_BITS = (4, 0, 3)
-NORM_MASKS = [
-    (b1 << 1) | (b2 << 2) | (b4 << 4) | (b5 << 5)
-    for b5 in (1, 0)
-    for b4 in (1, 0)
-    for b2 in (1, 0)
-    for b1 in (1, 0)
-    if b1 or b2 or b4 or b5
-]
+NORM_MASKS = [m for m in range(63, 0, -1) if not m >> SWAP_BITS[0] & 1]
+Z_MASK = 32
 LO_STEPS = sorted(
     [(dx, dz) for dx in range(8) for dz in range(2) if dx or dz],
     key=lambda s: -(min(s[0], 8 - s[0]) + 4 * s[1]),
@@ -67,11 +61,11 @@
 
 
 def kernel(
-    perm_ref, x_hbm, g_hbm, out_ref, norm_ref,
-    x, g, mats, work, rmat, prod,
+    count, perm_hbm, x_hbm, g_hbm, out_ref, norm_ref,
+    perm_ref, x, g, mats, work, rmat, prod,
     s1, a1, t1, s2, a2, t2, u2, stage, recv, f3, g3, k3,
     nsrc, nrecv, qsrc, qrecv,
-    load_sem, ssem, rsem, nssem, nrsem, assem, arsem, qssem, qrsem,
+    wave, ready, load_sem, ssem, rsem, nssem, nrsem, assem, arsem, qssem, qrsem,
 ):
     hi = lax.axis_index("hi")
     lo = lax.axis_index("lo")
@@ -89,19 +83,46 @@
     load_g0 = pltpu.make_async_copy(g_hbm.at[1], g.at[1], load_sem.at[1])
     load_ga = pltpu.make_async_copy(g_hbm.at[0], g.at[0], load_sem.at[2])
     load_gb = pltpu.make_async_copy(g_hbm.at[pl.ds(2, 14)], g.at[pl.ds(2, 14)], load_sem.at[3])
+    load_perm = pltpu.make_async_copy(perm_hbm, perm_ref, load_sem.at[4])
     load_g0.start()
     load_x.start()
+
+    z_bit = bit_of(hi, 5)
+    y_at = lax.rem(lax.div(hi, 2), 8)
+
+    def y_id(step):
+        return (hi + 2 * (lax.rem(y_at + step, 8) - y_at), lo)
+
+    around = [(hi, lo_peer(1, 0)), (hi, lo_peer(7, 0)), y_id(1), y_id(7)]
+    barrier = pltpu.get_barrier_semaphore()
+
+    def signal(sem, peer):
+        pl.semaphore_signal(sem, inc=1, device_id=peer, device_id_type=MESH)
+
+    signal(barrier, hi_id(1 << SWAP_BITS[0]))
+    for peer in around:
+        signal(barrier, peer)
+    signal(barrier, hi_id(1 << SWAP_BITS[1]))
+
+    @pl.when(z_at == 0)
+    def _():
+        signal(barrier, (hi, lo_peer(0, 1)))
+
+    @pl.when(z_bit == 0)
+    def _():
+        signal(barrier, hi_id(Z_MASK))
+
     load_gb.start()
     load_ga.start()
-
-    barrier = pltpu.get_barrier_semaphore()
-    hi_masks = NORM_MASKS + [1 << SWAP_BITS[1], 1 << SWAP_BITS[2]]
-    for dx, dz in LO_STEPS:
-        pl.semaphore_signal(
-            barrier, inc=1, device_id=(hi, lo_peer(dx, dz)), device_id_type=MESH
-        )
-    for mask in hi_masks:
-        pl.semaphore_signal(barrier, inc=1, device_id=hi_id(mask), device_id_type=MESH)
+    load_perm.start()
+
+    def tell():
+        for i, peer in enumerate(around):
+            signal(wave.at[i], peer)
+
+    def hear():
+        for i in range(4):
+            pl.semaphore_wait(wave.at[i], 1)
 
     def prepare(slot, gate):
         top, bottom = gate_matrix(g[gate, 0], g[gate, 1])
@@ -153,7 +174,7 @@
         )
 
     put_rows(s1, y)
-    pl.semaphore_wait(barrier, len(LO_STEPS) + len(hi_masks))
+    pl.semaphore_wait(barrier, 6 + z_at + z_bit)
 
     def half(side):
         return pl.ds(pl.multiple_of(side * 128, 128), 128)
@@ -161,18 +182,9 @@
     side = bit_of(hi, SWAP_BITS[0])
     send1 = exchange(s1.at[:, half(1 - side), :], a1, 0, 1 << SWAP_BITS[0])
     send1.start()
-    norm_sends = []
-    for i, mask in enumerate(NORM_MASKS):
-        copy = pltpu.make_async_remote_copy(
-            src_ref=nsrc.at[0],
-            dst_ref=nrecv.at[i],
-            send_sem=nssem.at[i],
-            recv_sem=nrsem.at[i],
-            device_id=hi_id(mask),
-            device_id_type=MESH,
-        )
-        copy.start()
-        norm_sends.append(copy)
+    nsend1 = exchange(nsrc.at[0], nrecv.at[0], 4, 1 << SWAP_BITS[0])
+    nsend1.start()
+    tell()
 
     def gate_mid(slot, read, ref, where):
         result = left(mats[slot], jnp.concatenate([read(0), read(1)], axis=0))
@@ -180,30 +192,51 @@
             ref[c, where, :] = result[c * 128 : (c + 1) * 128, :]
 
     load_gb.wait()
-    load_ga.wait()
     prepare(1, 2)
+    hear()
+    tell()
     gate_mid(1, lambda c: s1[c, half(side), :], t1, half(side))
+    hear()
+    tell()
     prepare(2, 5)
     prepare(3, 6)
     prepare(4, 9)
+    hear()
+    tell()
     for b in range(2):
         rows = pl.ds(b, 64, stride=2)
         top, bottom = gate_matrix(g.at[10, 0][rows, :], g.at[10, 1][rows, :])
         mats[5, b * 64 : (b + 1) * 64, :] = top
         mats[5, 128 + b * 64 : 128 + (b + 1) * 64, :] = bottom
-    prepare(6, 13)
-    prepare(7, 14)
-
-    prod[0:128, :] = g[0, 0]
-    prod[128:256, :] = g[0, 1]
-    for gate in (3, 4, 7, 8, 11, 12, 15):
-        top, bottom = gate_matrix(g[gate, 0], g[gate, 1])
-        work[0:128, :] = top
-        work[128:256, :] = bottom
-        prod[...] = left(work[...], prod[...])
-    top, bottom = gate_matrix(prod[0:128, :], prod[128:256, :])
-    rmat[0:128, :] = top
-    rmat[128:256, :] = bottom
+    hear()
+
+    @pl.when(z_at == 1)
+    def _():
+        signal(ready.at[0], (hi, lo_peer(0, 1)))
+
+    @pl.when(z_bit == 1)
+    def _():
+        signal(ready.at[1], hi_id(Z_MASK))
+
+    nsend1.wait()
+    qsrc[0] = nsrc[0] + nrecv[0]
+    qsends = []
+    for dx, dz in LO_STEPS:
+        qsends.append(
+            pltpu.make_async_remote_copy(
+                src_ref=qsrc.at[0],
+                dst_ref=qrecv.at[dx * 2 + dz],
+                send_sem=qssem.at[dx * 2 + dz],
+                recv_sem=qrsem.at[dx * 2 + dz],
+                device_id=(hi, lo_peer(dx, dz)),
+                device_id_type=MESH,
+            )
+        )
+
+    @pl.when(z_at == 1)
+    def _():
+        for copy in qsends:
+            copy.start()
 
     send1.wait()
     gate_mid(1, lambda c: a1[c], t1, half(1 - side))
@@ -212,19 +245,9 @@
     side = bit_of(hi, SWAP_BITS[1])
     send2 = exchange(s2.at[:, half(1 - side), :], a2, 1, 1 << SWAP_BITS[1])
     send2.start()
-    for copy in norm_sends:
-        copy.wait()
-    total = nsrc[0]
-    for i in range(len(NORM_MASKS)):
-        total = total + nrecv[i]
-    nsrc[1] = total
-    nsend2 = exchange(nsrc.at[1], nrecv.at[15], 4, 1 << SWAP_BITS[1])
-    nsend2.start()
     gate_mid(3, lambda c: s2[c, half(side), :], t2, half(side))
     send2.wait()
     gate_mid(3, lambda c: a2[c], t2, half(1 - side))
-    nsend2.wait()
-    qsrc[0] = nsrc[1] + nrecv[15]
 
     put_rows(t1, left(mats[4], get_rows(t2)))
     data = jnp.concatenate(
@@ -239,6 +262,7 @@
                     base : base + 64, t * 128 : (t + 1) * 128
                 ].reshape(8, 8, 128)
 
+    load_perm.wait()
     for j in range(16):
         block = jnp.int32(0)
         for v in range(1, 16):
@@ -246,6 +270,12 @@
         for b in range(2):
             for c in range(2):
                 stage[b, j, c] = u2[c, b, block]
+    @pl.when(z_at == 0)
+    def _():
+        pl.semaphore_wait(ready.at[0], 1)
+        for copy in qsends:
+            copy.start()
+
     sends = [[], []]
     for b in range(2):
         for dx, dz in LO_STEPS:
@@ -260,20 +290,47 @@
             )
             copy.start()
             sends[b].append(copy)
-    qsends = []
+    for b in range(2):
+        recv[b, lo] = stage[b, lo]
+
+    load_ga.wait()
+    prepare(6, 13)
+    prepare(7, 14)
+    prod[0:128, :] = g[0, 0]
+    prod[128:256, :] = g[0, 1]
+    for gate in (3, 4, 7, 8, 11, 12, 15):
+        top, bottom = gate_matrix(g[gate, 0], g[gate, 1])
+        work[0:128, :] = top
+        work[128:256, :] = bottom
+        prod[...] = left(work[...], prod[...])
+    top, bottom = gate_matrix(prod[0:128, :], prod[128:256, :])
+    rmat[0:128, :] = top
+    rmat[128:256, :] = bottom
+
+
+    total = qsrc[0]
+    for copy in qsends:
+        copy.wait()
     for dx, dz in LO_STEPS:
+        total = total + qrecv[dx * 2 + dz]
+    qsrc[1] = total
+
+    @pl.when(z_bit == 0)
+    def _():
+        pl.semaphore_wait(ready.at[1], 1)
+
+    norm_sends = []
+    for i, mask in enumerate(NORM_MASKS):
         copy = pltpu.make_async_remote_copy(
-            src_ref=qsrc.at[0],
-            dst_ref=qrecv.at[dx * 2 + dz],
-            send_sem=qssem.at[dx * 2 + dz],
-            recv_sem=qrsem.at[dx * 2 + dz],
-            device_id=(hi, lo_peer(dx, dz)),
+            src_ref=qsrc.at[1],
+            dst_ref=nrecv.at[1 + i],
+            send_sem=nssem.at[i],
+            recv_sem=nrsem.at[i],
+            device_id=hi_id(mask),
             device_id_type=MESH,
         )
         copy.start()
-        qsends.append(copy)
-    for b in range(2):
-        recv[b, lo] = stage[b, lo]
+        norm_sends.append(copy)
 
     side = bit_of(hi, SWAP_BITS[2])
 
@@ -293,15 +350,6 @@
         copy = exchange(f3.at[b, :, quarter(1 - side), :], g3.at[b], 2 + b, 1 << SWAP_BITS[2])
         copy.start()
         sends3.append(copy)
-    total = qsrc[0]
-    for copy in qsends:
-        copy.wait()
-    for dx, dz in LO_STEPS:
-        total = total + qrecv[dx * 2 + dz]
-    qsrc[1] = total
-    nsend3 = exchange(qsrc.at[1], qrecv.at[0], 5, 1 << SWAP_BITS[2])
-    nsend3.start()
-
     def finish(where):
         y = left(mats[7], jnp.concatenate([k3[0], k3[1]], axis=0))
         y = right(jnp.concatenate([y[0:128, :], y[128:256, :]], axis=1), rmat[...])
@@ -317,8 +365,13 @@
         for c in range(2):
             k3[c, pl.ds(b, 64, stride=2), :] = g3[b, c]
     finish(1 - side)
-    nsend3.wait()
-    norm_ref[...] = qsrc[1] + qrecv[0]
+    total = qsrc[1]
+    for copy in norm_sends:
+        copy.wait()
+    for i in range(len(NORM_MASKS)):
+        total = total + nrecv[1 + i]
+    mean_sq = jnp.sum(total, axis=1, keepdims=True) / count
+    norm_ref[...] = jnp.broadcast_to(1.0 / jnp.sqrt(mean_sq + 1e-06), (1, 128))
 
 
 def per_device(count, state, gates, remap_perm):
@@ -326,13 +379,10 @@
     vm = pltpu.VMEM
     dma = pltpu.SemaphoreType.DMA
     out, norm = pl.pallas_call(
-        kernel,
-        out_shape=(
-            jax.ShapeDtypeStruct((512, 128), F32),
-            jax.ShapeDtypeStruct((1, 128), F32),
-        ),
+        functools.partial(kernel, count),
+        out_shape=(vm((512, 128), F32), vm((1, 128), F32)),
         in_specs=[
-            pl.BlockSpec(memory_space=pltpu.SMEM),
+            pl.BlockSpec(memory_space=pl.ANY),
             pl.BlockSpec(memory_space=pl.ANY),
             pl.BlockSpec(memory_space=pl.ANY),
         ],
@@ -341,6 +391,7 @@
             pl.BlockSpec(memory_space=pltpu.VMEM),
         ),
         scratch_shapes=[
+            pltpu.SMEM((16,), jnp.int32),
             vm((512, 128), F32),
             vm((16, 2, 128, 128), F32),
             vm((8, 256, 768), BF16),
@@ -359,15 +410,17 @@
             vm((2, 2, 128, 128), F32),
             vm((2, 2, 64, 128), F32),
             vm((2, 128, 128), F32),
+            vm((1, 1, 128), F32),
+            vm((32, 1, 128), F32),
             vm((2, 1, 128), F32),
             vm((16, 1, 128), F32),
-            vm((2, 1, 128), F32),
-            vm((16, 1, 128), F32),
-            dma((4,)),
-            dma((6,)),
-            dma((6,)),
-            dma((15,)),
-            dma((15,)),
+            pltpu.SemaphoreType.REGULAR((4,)),
+            pltpu.SemaphoreType.REGULAR((2,)),
+            dma((5,)),
+            dma((5,)),
+            dma((5,)),
+            dma((31,)),
+            dma((31,)),
             dma((2, 16)),
             dma((2, 16)),
             dma((16,)),
@@ -375,9 +428,7 @@
         ],
         compiler_params=pltpu.CompilerParams(collective_id=0, has_side_effects=True),
     )(remap_perm, rows, gates)
-    mean_sq = jnp.sum(norm) / count
-    scaled = out * (1.0 / jnp.sqrt(mean_sq + 1e-06))
-    return scaled.reshape(256, 2, 128).transpose(1, 0, 2).reshape(2, 32768)
+    return (out * norm).reshape(256, 2, 128).transpose(1, 0, 2).reshape(2, 32768)
 
 
 def solution(mesh):

time: 54.1 us -> 47.2 us (0.87)
  Pallas kernels: 50.2 us -> 46.4 us
  other arithmetic: 2.94 us -> 0.72 us
  between operations: 0.7 us -> 0.01 us
    pallas_call x1, Pallas kernels: 50.2 us -> 46.4 us  [per_device(): pl.pallas_call(functools.partial(kernel, count), out_shape=(vm((512, 128)...]
    reduce_sum x1 -> x0, other arithmetic: 1.27 us -> none  [per_device(): mean_sq = jnp.sum(norm) / count]
    mul x1, other arithmetic: 1.67 us -> 0.72 us  [per_device(): out * norm]
where the time goes in v2:
time: 47.2 us; the launch traced here: 47.1 us
  Pallas kernels  46.4 us (98%)
  other arithmetic  0.72 us (2%)
    pallas_call x1, Pallas kernels, per_device(): pl.pallas_call(functools.partial(kernel, count), out_shape=(vm((512, 128)...  46.4 us

profile of v2, /device:TPU:2, one launch (start us, length us, event | category | flops | bytes accessed | tf_op | source)
XLA Modules:
  0.0 47.1 jit_solution(16054234716231772468)
XLA Ops:
  0.0 46.4 %shard_map.37 = (f32[512,128]{1,0:T(8,128)S(1)}, f32[1,128]{1,0:T(1,128)S(1)}) custom-call(s32[16]{0:T(128)} %perm_hbm.1, f32[512,128]{1,0:T(8,128)} %bitcast.12, f32[16,2,128,128]{3,2,1,0:T(8,128)} %g_hbm.1), custom_call_target="tpu_custom_call" | custom-call | tf_op jit(solution)/shard_map/pallas_call | solution.py:381
  46.4 0.7 %broadcast_multiply_fusion = f32[512,128]{1,0:T(8,128)} fusion(f32[512,128]{1,0:T(8,128)S(1)} %get-tuple-element.7, f32[128]{0:T(128)S(1)} %bitcast.11), kind=kLoop, calls=%fused_computation | loop fusion | flops 65536 | bytes 524800 | tf_op jit(solution)/shard_map/mul | solution.py:431

commit v3 on v2

--- a/solution.py
+++ b/solution.py
@@ -93,24 +93,27 @@
     def y_id(step):
         return (hi + 2 * (lax.rem(y_at + step, 8) - y_at), lo)
 
-    around = [(hi, lo_peer(1, 0)), (hi, lo_peer(7, 0)), y_id(1), y_id(7)]
+    around = [(hi, lo_peer(2, 0)), (hi, lo_peer(6, 0)), y_id(2), y_id(6)]
+    near = [(hi, lo_peer(1, 0)), (hi, lo_peer(7, 0)), y_id(1), y_id(7)]
     barrier = pltpu.get_barrier_semaphore()
 
     def signal(sem, peer):
         pl.semaphore_signal(sem, inc=1, device_id=peer, device_id_type=MESH)
 
     signal(barrier, hi_id(1 << SWAP_BITS[0]))
-    for peer in around:
+    for peer in around + near:
         signal(barrier, peer)
     signal(barrier, hi_id(1 << SWAP_BITS[1]))
 
     @pl.when(z_at == 0)
     def _():
-        signal(barrier, (hi, lo_peer(0, 1)))
+        for dx in range(8):
+            signal(barrier, (hi, lo_peer(dx, 1)))
 
     @pl.when(z_bit == 0)
     def _():
-        signal(barrier, hi_id(Z_MASK))
+        for y_mask in range(0, 16, 2):
+            signal(barrier, hi_id(Z_MASK | y_mask))
 
     load_gb.start()
     load_ga.start()
@@ -142,9 +145,6 @@
     load_g0.wait()
     prepare(0, 1)
     load_x.wait()
-
-    values = x[...].reshape(64, 8, 128)
-    nsrc[0] = jnp.sum(jnp.sum(values * values, axis=0), axis=0, keepdims=True)
 
     data = jnp.concatenate(
         [
@@ -174,7 +174,7 @@
         )
 
     put_rows(s1, y)
-    pl.semaphore_wait(barrier, 6 + z_at + z_bit)
+    pl.semaphore_wait(barrier, 10 + 8 * z_at + 8 * z_bit)
 
     def half(side):
         return pl.ds(pl.multiple_of(side * 128, 128), 128)
@@ -182,6 +182,9 @@
     side = bit_of(hi, SWAP_BITS[0])
     send1 = exchange(s1.at[:, half(1 - side), :], a1, 0, 1 << SWAP_BITS[0])
     send1.start()
+
+    values = x[...].reshape(64, 8, 128)
+    nsrc[0] = jnp.sum(jnp.sum(values * values, axis=0), axis=0, keepdims=True)
     nsend1 = exchange(nsrc.at[0], nrecv.at[0], 4, 1 << SWAP_BITS[0])
     nsend1.start()
     tell()
@@ -193,31 +196,15 @@
 
     load_gb.wait()
     prepare(1, 2)
-    hear()
-    tell()
     gate_mid(1, lambda c: s1[c, half(side), :], t1, half(side))
-    hear()
-    tell()
     prepare(2, 5)
     prepare(3, 6)
     prepare(4, 9)
-    hear()
-    tell()
     for b in range(2):
         rows = pl.ds(b, 64, stride=2)
         top, bottom = gate_matrix(g.at[10, 0][rows, :], g.at[10, 1][rows, :])
         mats[5, b * 64 : (b + 1) * 64, :] = top
         mats[5, 128 + b * 64 : 128 + (b + 1) * 64, :] = bottom
-    hear()
-
-    @pl.when(z_at == 1)
-    def _():
-        signal(ready.at[0], (hi, lo_peer(0, 1)))
-
-    @pl.when(z_bit == 1)
-    def _():
-        signal(ready.at[1], hi_id(Z_MASK))
-
     nsend1.wait()
     qsrc[0] = nsrc[0] + nrecv[0]
     qsends = []
@@ -233,11 +220,6 @@
             )
         )
 
-    @pl.when(z_at == 1)
-    def _():
-        for copy in qsends:
-            copy.start()
-
     send1.wait()
     gate_mid(1, lambda c: a1[c], t1, half(1 - side))
 
@@ -245,8 +227,22 @@
     side = bit_of(hi, SWAP_BITS[1])
     send2 = exchange(s2.at[:, half(1 - side), :], a2, 1, 1 << SWAP_BITS[1])
     send2.start()
+
+    hear()
+    signal(ready.at[2], hi_id(1 << SWAP_BITS[1]))
+
+    @pl.when(z_at == 1)
+    def _():
+        signal(ready.at[0], (hi, lo_peer(0, 1)))
+
+    @pl.when(z_at == 1)
+    def _():
+        for copy in qsends:
+            copy.start()
+
     gate_mid(3, lambda c: s2[c, half(side), :], t2, half(side))
     send2.wait()
+
     gate_mid(3, lambda c: a2[c], t2, half(1 - side))
 
     put_rows(t1, left(mats[4], get_rows(t2)))
@@ -270,17 +266,11 @@
         for b in range(2):
             for c in range(2):
                 stage[b, j, c] = u2[c, b, block]
-    @pl.when(z_at == 0)
-    def _():
-        pl.semaphore_wait(ready.at[0], 1)
-        for copy in qsends:
-            copy.start()
-
-    sends = [[], []]
+    sends = {}
     for b in range(2):
         for dx, dz in LO_STEPS:
             peer = lo_peer(dx, dz)
-            copy = pltpu.make_async_remote_copy(
+            sends[b, dx, dz] = pltpu.make_async_remote_copy(
                 src_ref=stage.at[b, peer],
                 dst_ref=recv.at[b, lo],
                 send_sem=assem.at[b, dx * 2 + dz],
@@ -288,10 +278,34 @@
                 device_id=(hi, peer),
                 device_id_type=MESH,
             )
+
+    def start(across):
+        for b in range(2):
+            for dx, dz in LO_STEPS:
+                if dz == across:
+                    sends[b, dx, dz].start()
+
+    @pl.when(z_at == 0)
+    def _():
+        start(0)
+        pl.semaphore_wait(ready.at[0], 1)
+        for copy in qsends:
             copy.start()
-            sends[b].append(copy)
+        start(1)
+
+    @pl.when(z_at == 1)
+    def _():
+        start(1)
+        start(0)
+
     for b in range(2):
         recv[b, lo] = stage[b, lo]
+
+    pl.semaphore_wait(ready.at[2], 1)
+
+    @pl.when(z_bit == 1)
+    def _():
+        signal(ready.at[1], hi_id(Z_MASK))
 
     load_ga.wait()
     prepare(6, 13)
@@ -339,8 +353,8 @@
 
     sends3 = []
     for b in range(2):
-        for copy in sends[b]:
-            copy.wait()
+        for dx, dz in LO_STEPS:
+            sends[b, dx, dz].wait()
         data = jnp.concatenate(
             [recv[b, :, 0].reshape(128, 128), recv[b, :, 1].reshape(128, 128)], axis=0
         )
@@ -415,7 +429,7 @@
             vm((2, 1, 128), F32),
             vm((16, 1, 128), F32),
             pltpu.SemaphoreType.REGULAR((4,)),
-            pltpu.SemaphoreType.REGULAR((2,)),
+            pltpu.SemaphoreType.REGULAR((3,)),
             dma((5,)),
             dma((5,)),
             dma((5,)),

time: 47.2 us -> 45.7 us (0.968)
  the two profiles are of different devices: /device:TPU:2 before, /device:TPU:16 now
where the time goes in v3:
time: 45.7 us; the launch traced here: 45.5 us
  Pallas kernels  44.8 us (98%)
  other arithmetic  0.72 us (2%)
    pallas_call x1, Pallas kernels, per_device(): pl.pallas_call(functools.partial(kernel, count), out_shape=(vm((512, 128)...  44.8 us

profile of v3, /device:TPU:16, one launch (start us, length us, event | category | flops | bytes accessed | tf_op | source)
XLA Modules:
  0.0 45.5 jit_solution(14702116432916728660)
XLA Ops:
  0.0 44.8 %shard_map.37 = (f32[512,128]{1,0:T(8,128)S(1)}, f32[1,128]{1,0:T(1,128)S(1)}) custom-call(s32[16]{0:T(128)} %perm_hbm.1, f32[512,128]{1,0:T(8,128)} %bitcast.12, f32[16,2,128,128]{3,2,1,0:T(8,128)} %g_hbm.1), custom_call_target="tpu_custom_call" | custom-call | tf_op jit(solution)/shard_map/pallas_call | solution.py:395
  44.8 0.7 %broadcast_multiply_fusion = f32[512,128]{1,0:T(8,128)} fusion(f32[512,128]{1,0:T(8,128)S(1)} %get-tuple-element.7, f32[128]{0:T(128)S(1)} %bitcast.11), kind=kLoop, calls=%fused_computation | loop fusion | flops 65536 | bytes 524800 | tf_op jit(solution)/shard_map/mul | solution.py:445

commit v4 on v3

--- a/solution.py
+++ b/solution.py
@@ -86,6 +86,9 @@
     load_perm = pltpu.make_async_copy(perm_hbm, perm_ref, load_sem.at[4])
     load_g0.start()
     load_x.start()
+    load_perm.start()
+    load_gb.start()
+    load_ga.start()
 
     z_bit = bit_of(hi, 5)
     y_at = lax.rem(lax.div(hi, 2), 8)
@@ -114,10 +117,6 @@
     def _():
         for y_mask in range(0, 16, 2):
             signal(barrier, hi_id(Z_MASK | y_mask))
-
-    load_gb.start()
-    load_ga.start()
-    load_perm.start()
 
     def tell():
         for i, peer in enumerate(around):
@@ -205,6 +204,13 @@
         top, bottom = gate_matrix(g.at[10, 0][rows, :], g.at[10, 1][rows, :])
         mats[5, b * 64 : (b + 1) * 64, :] = top
         mats[5, 128 + b * 64 : 128 + (b + 1) * 64, :] = bottom
+    load_perm.wait()
+    blocks = []
+    for j in range(16):
+        block = jnp.int32(0)
+        for v in range(1, 16):
+            block = jnp.where(perm_ref[v] == j, v, block)
+        blocks.append(block)
     nsend1.wait()
     qsrc[0] = nsrc[0] + nrecv[0]
     qsends = []
@@ -258,14 +264,10 @@
                     base : base + 64, t * 128 : (t + 1) * 128
                 ].reshape(8, 8, 128)
 
-    load_perm.wait()
     for j in range(16):
-        block = jnp.int32(0)
-        for v in range(1, 16):
-            block = jnp.where(perm_ref[v] == j, v, block)
         for b in range(2):
             for c in range(2):
-                stage[b, j, c] = u2[c, b, block]
+                stage[b, j, c] = u2[c, b, blocks[j]]
     sends = {}
     for b in range(2):
         for dx, dz in LO_STEPS:
@@ -364,20 +366,22 @@
         copy = exchange(f3.at[b, :, quarter(1 - side), :], g3.at[b], 2 + b, 1 << SWAP_BITS[2])
         copy.start()
         sends3.append(copy)
+    def low_bits(b, read):
+        y = right(jnp.concatenate([read(0), read(1)], axis=1), rmat[...])
+        for c in range(2):
+            k3[c, pl.ds(b, 64, stride=2), :] = y[:, c * 128 : (c + 1) * 128]
+
     def finish(where):
         y = left(mats[7], jnp.concatenate([k3[0], k3[1]], axis=0))
-        y = right(jnp.concatenate([y[0:128, :], y[128:256, :]], axis=1), rmat[...])
         for c in range(2):
-            out_ref[pl.ds(where * 256 + c, 128, stride=2), :] = y[:, c * 128 : (c + 1) * 128]
-
-    for b in range(2):
-        for c in range(2):
-            k3[c, pl.ds(b, 64, stride=2), :] = f3[b, c, quarter(side), :]
+            out_ref[pl.ds(where * 256 + c, 128, stride=2), :] = y[c * 128 : (c + 1) * 128, :]
+
+    for b in range(2):
+        low_bits(b, lambda c: f3[b, c, quarter(side), :])
     finish(side)
     for b in range(2):
         sends3[b].wait()
-        for c in range(2):
-            k3[c, pl.ds(b, 64, stride=2), :] = g3[b, c]
+        low_bits(b, lambda c: g3[b, c])
     finish(1 - side)
     total = qsrc[1]
     for copy in norm_sends:

time: 45.7 us -> 45.6 us (level)
  the two profiles are of different devices: /device:TPU:16 before, /device:TPU:2 now
where the time goes in v4:
time: 45.6 us; the launch traced here: 45.4 us
  Pallas kernels  44.7 us (98%)
  other arithmetic  0.72 us (2%)
    pallas_call x1, Pallas kernels, per_device(): pl.pallas_call(functools.partial(kernel, count), out_shape=(vm((512, 128)...  44.7 us

profile of v4, /device:TPU:2, one launch (start us, length us, event | category | flops | bytes accessed | tf_op | source)
XLA Modules:
  0.0 45.4 jit_solution(2071978986120509890)
XLA Ops:
  0.0 44.7 %shard_map.37 = (f32[512,128]{1,0:T(8,128)S(1)}, f32[1,128]{1,0:T(1,128)S(1)}) custom-call(s32[16]{0:T(128)} %perm_hbm.1, f32[512,128]{1,0:T(8,128)} %bitcast.12, f32[16,2,128,128]{3,2,1,0:T(8,128)} %g_hbm.1), custom_call_target="tpu_custom_call" | custom-call | tf_op jit(solution)/shard_map/pallas_call | solution.py:399
  44.7 0.7 %broadcast_multiply_fusion = f32[512,128]{1,0:T(8,128)} fusion(f32[512,128]{1,0:T(8,128)S(1)} %get-tuple-element.7, f32[128]{0:T(128)S(1)} %bitcast.11), kind=kLoop, calls=%fused_computation | loop fusion | flops 65536 | bytes 524800 | tf_op jit(solution)/shard_map/mul | solution.py:449
